TPU v7x, 32 devices: a whole 2x2x4 slice. The times are simulated.
32 devices in a mesh: leaf: 4 (over y, core), panel: 8 (over z, x).
Axes of the slice: x: 2, y: 2, z: 4, core: 2. Of those that a mesh axis runs over, the one named last changes fastest.
Arguments:
- pivot_rhs: float32 [4, 48, 4096], P('leaf', None, 'panel'), may hold values from -6 to 6
- subtree_update: float32 [4, 64, 4096], P('leaf', None, 'panel'), may hold values from -6 to 6
- lower_pivot: bfloat16 [2, 4, 4096, 4096], P(None, 'leaf', 'panel'), as said below
- lower_update: bfloat16 [2, 4, 4096, 4096], P(None, 'leaf', None, 'panel'), as said below
- row_map: int32 [2, 4, 2, 4096], P(None, 'leaf', None, 'panel'), may hold values from 0 to 1023, as said below
- root_inverse: bfloat16 [4096, 4096], P('panel'), as said below
Outputs:
- pivot_solution: float32 [4, 48, 4096], P('leaf', None, 'panel')
- subtree_solution: float32 [4, 64, 4096], P('leaf', None, 'panel')
Inputs may be any that keep to these rules, and one draw needn't show every extreme that they name: row_map[l, i] is the same for all i that share i >> (l + 1); within one panel block of 512 rows of one child the values are distinct. lower_pivot[l, i] is the same for all i that share i >> (l + 1), and is zero above its diagonal blocks of 512 rows. lower_update[l, i] is the same for all i that share i >> (l + 1). root_inverse is symmetric.
All inputs are finite; a program needn't handle non-finite values.
Results may differ from a plain program's by a relative error of at most 0.0003.
Values sent between devices are 32-bit elements; how exact they have to be, the bound alone decides.
A program may use at most 64 MiB of HBM per device.

v0:
```python
import jax
import jax.numpy as jnp
from jax import lax
from jax.sharding import PartitionSpec as P

HIGHEST_PRECISION = lax.Precision.HIGHEST
CONTRACT_LAST = (((1,), (1,)), ((), ()))
CONTRACT_FIRST_LAST = (((0,), (1,)), ((), ()))


def partner(value, axis, stride):
    return lax.ppermute(value, axis, [(i, i ^ 1 << stride) for i in range(lax.axis_size(axis))])


def local(pivot_rhs, subtree_update, lower_pivot, lower_update, row_map, root_inverse):
    levels = lax.axis_size("leaf").bit_length() - 1
    leaf_index = lax.axis_index("leaf")
    pivot_block = pivot_rhs.shape[2]
    update_block = subtree_update.shape[2]
    slot_count = pivot_block + update_block
    current = subtree_update[0]
    solved_levels = []
    onehot_tables = []
    leaf_bits = []
    offset = 0
    for tree_level in range(levels):
        leaf_bit = leaf_index >> tree_level & 1
        col_count = current.shape[0] // 2
        halves = current.reshape(col_count, 2, update_block)
        kept_half = jnp.where(leaf_bit == 0, halves[:, 0], halves[:, 1])
        sent_half = jnp.where(leaf_bit == 0, halves[:, 1], halves[:, 0])
        received = partner(sent_half, "leaf", tree_level)
        children = jnp.where(
            leaf_bit == 0,
            jnp.concatenate([kept_half, received], 1),
            jnp.concatenate([received, kept_half], 1),
        )
        maps = row_map[tree_level, 0].reshape(2 * update_block)
        onehot_table = (maps[:, None] == jnp.arange(slot_count, dtype=jnp.int32)[None, :]).astype(
            jnp.float32
        )
        assembled = jnp.dot(children, onehot_table, precision=HIGHEST_PRECISION)
        right_side = pivot_rhs[0, offset : offset + col_count] + assembled[:, :pivot_block]
        offset = offset + col_count
        inverse_rows = lower_pivot[tree_level, 0]
        update_cols = lower_update[tree_level, 0]
        inverse_cols = inverse_rows.astype(jnp.float32)
        solved = lax.dot_general(
            lax.all_gather(right_side, "panel", axis=1, tiled=True),
            inverse_cols,
            CONTRACT_LAST,
            precision=HIGHEST_PRECISION,
        )
        factor_rows = update_cols.astype(jnp.float32)
        coupled_update = lax.psum_scatter(
            lax.dot_general(factor_rows, solved, CONTRACT_LAST, precision=HIGHEST_PRECISION),
            "panel",
            scatter_dimension=0,
            tiled=True,
        ).T
        current = assembled[:, pivot_block:] - coupled_update
        solved_levels.append(solved)
        onehot_tables.append(onehot_table)
        leaf_bits.append(leaf_bit)
    root_inverse_cols = root_inverse.astype(jnp.float32)
    known = lax.dot_general(
        lax.all_gather(current, "panel", axis=1, tiled=True),
        root_inverse_cols,
        CONTRACT_LAST,
        precision=HIGHEST_PRECISION,
    )
    pieces = [None] * levels
    for tree_level in range(levels - 1, -1, -1):
        inverse_rows = lower_pivot[tree_level, 0]
        update_cols = lower_update[tree_level, 0]
        forward_part = solved_levels[tree_level]
        col_count = forward_part.shape[0]
        known_factor_rows = update_cols.astype(jnp.float32)
        coupling = jnp.dot(
            lax.all_gather(known, "panel", axis=1, tiled=True),
            known_factor_rows,
            precision=HIGHEST_PRECISION,
        )
        residual_part = forward_part - coupling
        pivot_inverse_cols = inverse_rows.astype(jnp.float32)
        own_x = lax.psum_scatter(
            lax.dot_general(
                pivot_inverse_cols, residual_part, CONTRACT_FIRST_LAST, precision=HIGHEST_PRECISION
            ),
            "panel",
            scatter_dimension=0,
            tiled=True,
        ).T
        pieces[tree_level] = own_x
        whole_front = jnp.concatenate([own_x, known], 1)
        children = lax.dot_general(
            whole_front, onehot_tables[tree_level], CONTRACT_LAST, precision=HIGHEST_PRECISION
        )
        leaf_bit = leaf_bits[tree_level]
        first_child = children[:, :update_block]
        second_child = children[:, update_block:]
        own_child = jnp.where(leaf_bit == 0, first_child, second_child)
        sent_child = jnp.where(leaf_bit == 0, second_child, first_child)
        received = partner(sent_child, "leaf", tree_level)
        paired = jnp.where(
            leaf_bit == 0, jnp.stack([own_child, received], 1), jnp.stack([received, own_child], 1)
        )
        known = paired.reshape(2 * col_count, update_block)
    return (jnp.concatenate(pieces, 0)[None], known[None])


def solution(mesh):
    in_specs = (
        P("leaf", None, "panel"),
        P("leaf", None, "panel"),
        P(None, "leaf", "panel", None),
        P(None, "leaf", None, "panel"),
        P(None, "leaf", None, "panel"),
        P("panel", None),
    )
    out_specs = (P("leaf", None, "panel"), P("leaf", None, "panel"))
    return jax.shard_map(local, mesh=mesh, in_specs=in_specs, out_specs=out_specs, check_vma=False)
```

profile of v0, /device:TPU:0, one launch (start us, length us, event | category | flops | bytes accessed | tf_op | source)
XLA Modules:
  0.0 490.2 jit_solution(4684953163303562873)
XLA Ops:
  7.2 1.0 reshape_squeeze.3
  9.8 1.6 fusion.15
  11.4 0.9 slice_add_fusion
  12.3 33.1 %all_gather.15 = f32[32,4096]{1,0:T(8,128)S(1)} all-gather(f32[32,512]{1,0:T(8,128)S(1)} %slice_add_fusion), channel_id=1, replica_groups=mesh['leaf'=4,'panel'=8] {'panel'}, dimensions={1}, use_global_device_ids=true | all-gather | bytes 589824 | tf_op jit(solution)/shard_map/all_gather | solution.py:49
  45.4 5.9 %fusion.10 = f32[32,512]{1,0:T(8,128)S(1)} fusion(f32[32,4096]{1,0:T(8,128)S(1)} %all_gather.15, bf16[2,1,512,4096]{3,2,1,0:T(8,128)(2,1)} %param.8), kind=kOutput, calls=%fused_computation.14 | convolution fusion | flops 805306368 | bytes 4784128 | tf_op jit(solution)/shard_map/dot_general | solution.py:48
  51.3 6.7 %convolution_bitcast_fusion.1 = f32[4096,32]{0,1:T(8,128)} fusion(f32[32,512]{1,0:T(8,128)S(1)} %fusion.10, bf16[2,1,4096,512]{3,2,1,0:T(8,128)(2,1)} %param.9), kind=kOutput, calls=%fused_computation.1 | convolution fusion | flops 805306368 | bytes 4784128 | tf_op jit(solution)/shard_map/dot_general | solution.py:56
  58.0 63.3 %reduce-scatter.5.cloned.1.call-done = f32[512,32]{0,1:T(8,128)} async-done(((f32[4096,32]{0,1:T(8,128)}), f32[512,32]{0,1:T(8,128)}) %reduce-scatter.5.cloned.1.call-update) | async-done | bytes 65552 | tf_op jit(solution)/shard_map/reduce_scatter | solution.py:55
  121.3 0.8 slice_subtract_fusion
  122.3 1.6 collective-permute-start.1
  123.8 2.4 collective-permute-done.1
  126.3 1.5 fusion.13
  127.7 0.8 slice_add_fusion.1
  128.5 30.9 %all_gather.16 = f32[16,4096]{1,0:T(8,128)S(1)} all-gather(f32[16,512]{1,0:T(8,128)S(1)} %slice_add_fusion.1), channel_id=1, replica_groups=mesh['leaf'=4,'panel'=8] {'panel'}, dimensions={1}, use_global_device_ids=true | all-gather | bytes 294912 | tf_op jit(solution)/shard_map/all_gather | solution.py:49
  159.4 5.5 %fusion.4 = f32[16,512]{1,0:T(8,128)S(1)} fusion(f32[16,4096]{1,0:T(8,128)S(1)} %all_gather.16, bf16[2,1,512,4096]{3,2,1,0:T(8,128)(2,1)} %param.8), kind=kOutput, calls=%fused_computation.8 | convolution fusion | flops 402653184 | bytes 4489216 | tf_op jit(solution)/shard_map/dot_general | solution.py:48
  165.0 6.3 %convolution_bitcast_fusion.3 = f32[4096,16]{0,1:T(8,128)} fusion(f32[16,512]{1,0:T(8,128)S(1)} %fusion.4, bf16[2,1,4096,512]{3,2,1,0:T(8,128)(2,1)} %param.9), kind=kOutput, calls=%fused_computation.3 | convolution fusion | flops 402653184 | bytes 4489216 | tf_op jit(solution)/shard_map/dot_general | solution.py:56
  171.3 60.5 %reduce-scatter.7.cloned.1.call-done = f32[512,16]{0,1:T(8,128)} async-done(((f32[4096,16]{0,1:T(8,128)}), f32[512,16]{0,1:T(8,128)}) %reduce-scatter.7.cloned.1.call-update) | async-done | bytes 32784 | tf_op jit(solution)/shard_map/reduce_scatter | solution.py:55
  231.8 0.8 slice_subtract_fusion.1
  232.5 30.9 %all_gather.17 = f32[16,4096]{1,0:T(8,128)S(1)} all-gather(f32[16,512]{1,0:T(8,128)S(1)} %slice_subtract_fusion.1), channel_id=1, replica_groups=mesh['leaf'=4,'panel'=8] {'panel'}, dimensions={1}, use_global_device_ids=true | all-gather | bytes 294912 | tf_op jit(solution)/shard_map/all_gather | solution.py:67
  263.4 5.5 %fusion.60 = f32[16,512]{1,0:T(8,128)S(1)} fusion(f32[16,4096]{1,0:T(8,128)S(1)} %all_gather.17, bf16[512,4096]{1,0:T(8,128)(2,1)} %param.11), kind=kOutput, calls=%fused_computation.83 | convolution fusion | flops 402653184 | bytes 4489216 | tf_op jit(solution)/shard_map/dot_general | solution.py:66
  269.0 30.8 %all_gather.18 = f32[16,4096]{1,0:T(8,128)S(1)} all-gather(f32[16,512]{1,0:T(8,128)S(1)} %fusion.60), channel_id=1, replica_groups=mesh['leaf'=4,'panel'=8] {'panel'}, dimensions={1}, use_global_device_ids=true | all-gather | bytes 294912 | tf_op jit(solution)/shard_map/all_gather | solution.py:80
  299.7 3.9 fusion.31
  303.6 4.7 convolution_bitcast_fusion.2
  308.4 60.5 %reduce-scatter.9.cloned.1.call-done = f32[512,16]{0,1:T(8,128)} async-done(((f32[4096,16]{0,1:T(8,128)}), f32[512,16]{0,1:T(8,128)}) %reduce-scatter.9.cloned.1.call-update) | async-done | bytes 32784 | tf_op jit(solution)/shard_map/reduce_scatter | solution.py:86
  368.8 2.8 fusion.12
  371.6 1.6 collective-permute-start.2
  373.2 2.4 collective-permute-done.2
  375.7 31.5 %all_gather.19 = f32[32,4096]{1,0:T(8,128)S(1)} all-gather(f32[32,512]{1,0:T(8,128)S(1)} %select_n.121), channel_id=1, replica_groups=mesh['leaf'=4,'panel'=8] {'panel'}, dimensions={1}, use_global_device_ids=true | all-gather | bytes 589824 | tf_op jit(solution)/shard_map/all_gather | solution.py:80
  407.2 4.3 fusion.28
  411.5 5.1 %convolution_bitcast_fusion = f32[4096,32]{0,1:T(8,128)} fusion(f32[32,512]{1,0:T(8,128)S(1)} %fusion.28, bf16[2,1,512,4096]{3,2,1,0:T(8,128)(2,1)} %param.8), kind=kOutput, calls=%fused_computation | convolution fusion | flops 805306368 | bytes 4784128 | tf_op jit(solution)/shard_map/dot_general | solution.py:87
  416.7 61.5 %reduce-scatter.11.cloned.1.call-done = f32[512,32]{0,1:T(8,128)} async-done(((f32[4096,32]{0,1:T(8,128)}), f32[512,32]{0,1:T(8,128)}) %reduce-scatter.11.cloned.1.call-update) | async-done | bytes 65552 | tf_op jit(solution)/shard_map/reduce_scatter | solution.py:86
  478.2 3.0 fusion.14
  481.3 1.5 maximum_bitcast_fusion
  (32 shorter events, 3.0 us)
Async XLA Ops:
  7.2 114.1 %reduce-scatter.5.cloned.1.call-start = ((), (), s32[]{:S(2)}) async-start(), calls=%async_computation.4 | async-start | bytes 589824 | tf_op jit(solution)/shard_map/reduce_scatter | solution.py:55
  8.3 1.4 collective-permute-start
  57.9 173.8 %reduce-scatter.7.cloned.1.call-start = ((), (), s32[]{:S(2)}) async-start(), calls=%async_computation.5 | async-start | bytes 294912 | tf_op jit(solution)/shard_map/reduce_scatter | solution.py:55
  122.3 4.0 collective-permute-start.1
  171.2 197.6 %reduce-scatter.9.cloned.1.call-start = ((), (), s32[]{:S(2)}) async-start(), calls=%async_computation.6 | async-start | bytes 294912 | tf_op jit(solution)/shard_map/reduce_scatter | solution.py:86
  308.3 169.9 %reduce-scatter.11.cloned.1.call-start = ((), (), s32[]{:S(2)}) async-start(), calls=%async_computation.7 | async-start | bytes 589824 | tf_op jit(solution)/shard_map/reduce_scatter | solution.py:86
  371.6 4.0 collective-permute-start.2
  411.5 69.8 %copy-start = (f32[512,16]{0,1:T(8,128)S(1)}, f32[512,16]{0,1:T(8,128)}, u32[]{:S(2)}) copy-start(f32[512,16]{0,1:T(8,128)} %reduce-scatter.9.cloned.1.call-done) | copy-start | bytes 98308
  481.2 1.6 collective-permute-start.3
Sparse Core Ops, SparseCore 0:
  58.1 63.1 reduce-scatter.4
  171.4 60.3 reduce-scatter.6
  308.4 60.3 reduce-scatter.8
  416.8 61.3 reduce-scatter.10
where the time goes:
time: 491 us; the launch traced here: 490 us
  waiting for transfers between devices  251 us (51%)
  blocking collectives  157 us (32%)
  matrix products  56.8 us (12%)
  between operations  13.9 us (3%)
  other arithmetic  4.96 us (1%)
    reduce_scatter x2, waiting for transfers between devices, local(): lax.psum_scatter(lax.dot_general(factor_rows, solved, CONTRACT_LAST, prec...  124 us
    reduce_scatter x2, waiting for transfers between devices, local(): lax.psum_scatter(lax.dot_general(pivot_inverse_cols, residual_part, CONTR...  122 us
    all_gather x2, blocking collectives, local(): lax.all_gather(right_side, 'panel', axis=1, tiled=True)  64 us
    all_gather x2, blocking collectives, local(): lax.all_gather(known, 'panel', axis=1, tiled=True)  62.2 us
    all_gather x1, blocking collectives, local(): lax.all_gather(current, 'panel', axis=1, tiled=True)  30.9 us
    dot_general x2, matrix products, local(): lax.dot_general(factor_rows, solved, CONTRACT_LAST, precision=HIGHEST_PRE...  12.9 us
    dot_general x2, matrix products, local(): lax.dot_general(lax.all_gather(right_side, 'panel', axis=1, tiled=True),...  11.4 us
  transfers between devices with their start and end apart: 8, of which 7 were waited for; matrix products, arithmetic and copies ran while one was open for 0% of the time, Pallas kernels for 0%

commit v1 on v0

v1 whole, which is shorter than its diff:
```python
import functools

import jax
import jax.numpy as jnp
from jax import lax
from jax.experimental import pallas as pl
from jax.experimental.pallas import tpu as pltpu
from jax.sharding import PartitionSpec as P

MESH = pl.DeviceIdType.MESH
OUTER_MAX = 4
NT = (((1,), (1,)), ((), ()))
NN = (((1,), (0,)), ((), ()))


def bit_reverse(value, bits):
    out = 0
    for i in range(bits):
        out |= (value >> i & 1) << (bits - 1 - i)
    return out


def split(x):
    high = x.astype(jnp.bfloat16).astype(jnp.float32)
    return jnp.concatenate([high, x - high], 0).astype(jnp.bfloat16)


def fold(x):
    half = x.shape[0] // 2
    return x[:half] + x[half:]


def dot(x, w, dims):
    return lax.dot_general(x, w, dims, preferred_element_type=jnp.float32)


def loop(low, high, step, carry):
    if high - low <= 2:
        for i in range(low, high):
            carry = step(i, carry)
        return carry
    return lax.fori_loop(low, high, step, carry)


def kernel(levels, outer, inner, names, *args):
    ref = dict(zip(names, args))
    pivot_in, update_in, maps = ref["pivot_rhs"], ref["subtree_update"], ref["row_map"]
    pivot_out, update_out = ref["pivot_solution"], ref["subtree_solution"]
    pivots, updates, root = ref["pivots"], ref["updates"], ref["root"]
    panels = outer * inner
    pivot_block, update_block = pivot_in.shape[2], update_in.shape[2]
    vectors = update_in.shape[1]
    slots = pivot_block + update_block
    group = vectors >> levels

    leaf = lax.axis_index("leaf")
    panel = lax.axis_index("panel")
    row, col = panel // inner, panel % inner

    bits = [(leaf >> level) & 1 for level in range(levels)]
    counts = [vectors >> (level + 1) for level in range(levels)]
    offsets = [sum(counts[:level]) for level in range(levels)]

    loads = []
    for level in range(levels):
        loads.append(pltpu.make_async_copy(
            ref["lower_pivot"].at[level, 0], pivots.at[level], ref["load_sem"].at[2 * level]))
        loads.append(pltpu.make_async_copy(
            ref["lower_update"].at[level, 0], updates.at[level], ref["load_sem"].at[2 * level + 1]))
    loads.append(pltpu.make_async_copy(ref["root_inverse"], root, ref["load_sem"].at[2 * levels]))
    for load in loads:
        load.start()

    barrier = pltpu.get_barrier_semaphore()
    for d in range(1, outer):
        pl.semaphore_signal(barrier, 1, device_id={"panel": (row ^ d) * inner + col}, device_id_type=MESH)
    for e in range(1, inner):
        pl.semaphore_signal(barrier, 1, device_id={"panel": row * inner + (col ^ e)}, device_id_type=MESH)
    for level in range(levels):
        pl.semaphore_signal(barrier, 1, device_id={"leaf": leaf ^ (1 << level)}, device_id_type=MESH)

    first = ref["current0"]
    for g in range(1 << levels):
        for k in range(group):
            first[pl.ds(g * group + k, 1), :] = update_in[0, pl.ds(k << levels | bit_reverse(g, levels), 1), :]
    for level in range(levels):
        size = levels - 1 - level
        for g in range(1 << size):
            for k in range(group):
                ref["rhs%d" % level][pl.ds(g * group + k, 1), :] = pivot_in[
                    0, pl.ds(offsets[level] + (k << size | bit_reverse(g, size)), 1), :]
    pl.semaphore_wait(barrier, outer - 1 + inner - 1 + levels)

    row_order = [d for d in (1, 3, 2) if d < outer]
    far_order = [d for d in (3, 2, 1) if d < outer]

    def place(d, e):
        return (row ^ d) * inner + (col ^ e)

    def send(source, target, which, slot, device):
        return pltpu.make_async_remote_copy(
            src_ref=source, dst_ref=target, send_sem=ref["send_sem"].at[which, slot],
            recv_sem=ref["recv_sem"].at[which, slot], device_id=device, device_id_type=MESH)

    def to_row(source, target, which, slot, d):
        return send(source, target, which, slot, {"panel": (row ^ d) * inner + col})

    def to_col(source, target, which, slot, e):
        return send(source, target, which, slot, {"panel": row * inner + (col ^ e)})

    def gather(which, buf, value, use, acc):
        buf[0] = value
        for d in far_order:
            to_row(buf.at[0], buf.at[d * inner], which, d * inner, d).start()

        def forward(d):
            def go(e, _):
                to_col(buf.at[d * inner], buf.at[d * inner + e], which, d * inner + e, e).start()
                return _
            loop(1, inner, go, 0)

        def arrived(d, acc):
            def go(e, acc):
                slot = d * inner + e
                to_col(buf.at[slot], buf.at[slot], which, slot, e).wait_recv()
                return use(acc, buf[slot], place(d, e))
            return loop(1, inner, go, acc)

        forward(0)
        acc = use(acc, buf[0], place(0, 0))
        last = 0
        for d in row_order:
            to_row(buf.at[d * inner], buf.at[d * inner], which, d * inner, d).wait_recv()
            forward(d)
            acc = use(acc, buf[d * inner], place(d, 0))
            acc = arrived(last, acc)
            last = d
        return arrived(last, acc)

    def scatter(which, part_buf, in_buf, part):
        for d in far_order + [0]:
            def go(e, _, d=d):
                slot = d * inner + e
                part_buf[slot] = part(place(d, e))
                to_col(part_buf.at[slot], in_buf.at[slot], which, slot, e).start()
                return _
            loop(1, inner, go, 0)

        def collect(d):
            def go(e, acc):
                slot = d * inner + e
                to_col(in_buf.at[slot], in_buf.at[slot], which, slot, e).wait_recv()
                return acc + in_buf[slot]
            return loop(1, inner, go, part(place(d, 0)))

        for d in far_order:
            slot = d * inner
            part_buf[slot] = collect(d)
            to_row(part_buf.at[slot], in_buf.at[slot], which, slot, d).start()
        acc = collect(0)
        for d in row_order:
            slot = d * inner
            to_row(in_buf.at[slot], in_buf.at[slot], which, slot, d).wait_recv()
            acc = acc + in_buf[slot]
        return acc

    def swap(source, target, which, level):
        return pltpu.make_async_remote_copy(
            src_ref=source, dst_ref=target, send_sem=ref["swap_send_sem"].at[which],
            recv_sem=ref["swap_recv_sem"].at[which], device_id={"leaf": leaf ^ (1 << level)},
            device_id_type=MESH)

    def block_of(index, size):
        return pl.ds(pl.multiple_of(index * size, size), size)

    swaps = []

    def begin_swap(level):
        count = counts[level]
        copy = swap(ref["current%d" % level].at[block_of(1 - bits[level], count)],
                    ref["swapped%d" % level], level, level)
        copy.start()
        swaps.append(copy)
        return copy

    copy = begin_swap(0)

    chunk = min(128, slots)
    for level in range(levels):
        for side in range(2):
            child = bits[level] if side == 0 else 1 - bits[level]
            target = maps[level, 0, pl.ds(child, 1), :]

            def fill(i, _, level=level, side=side, target=target):
                rows = lax.broadcasted_iota(jnp.int32, (chunk, update_block), 0) + i * chunk
                ref["tables"][level, side, block_of(i, chunk), :] = jnp.where(
                    rows == target, 1.0, 0.0).astype(jnp.bfloat16)
                return _
            lax.fori_loop(0, slots // chunk, fill, 0)

    tables = ref["tables"]
    for level in range(levels):
        count = counts[level]
        current = ref["current%d" % level]
        if level:
            copy = begin_swap(level)
        total = dot(split(current[block_of(bits[level], count), :]), tables[level, 0], NT)
        copy.wait_recv()
        total = total + dot(split(ref["swapped%d" % level][...]), tables[level, 1], NT)
        assembled = fold(total)
        ref["kept%d" % level][...] = assembled[:, pivot_block:]
        loads[2 * level].wait()

        def use(acc, value, index, level=level):
            return acc + dot(split(value), pivots[level, :, block_of(index, pivot_block)], NT)

        solved = fold(gather(2 * level, ref["gather%d" % (2 * level)],
                             ref["rhs%d" % level][...] + assembled[:, :pivot_block], use, jnp.zeros((2 * count, pivot_block), jnp.float32)))
        ref["solved%d" % level][...] = solved
        pair = ref["pair%d" % level]
        pair[...] = split(solved)
        loads[2 * level + 1].wait()

        def part(index, level=level, pair=pair):
            return fold(dot(pair[...], updates[level, block_of(index, update_block), :], NT))

        coupled = scatter(2 * level + 1, ref["part%d" % (2 * level + 1)], ref["land%d" % (2 * level + 1)], part)
        ref["current%d" % (level + 1)][...] = ref["kept%d" % level][...] - coupled

    loads[2 * levels].wait()
    count = counts[levels - 1]

    def use_root(acc, value, index):
        return acc + dot(split(value), root[:, block_of(index, update_block)], NT)

    known = fold(gather(2 * levels, ref["gather%d" % (2 * levels)], ref["current%d" % levels][...],
                        use_root, jnp.zeros((2 * count, update_block), jnp.float32)))
    ref["known%d" % levels][...] = known

    for level in range(levels - 1, -1, -1):
        count = counts[level]
        which = 2 * levels + 1 + 2 * level
        known = ref["known%d" % (level + 1)]

        def use(acc, value, index, level=level):
            return acc + dot(split(value), updates[level, block_of(index, update_block), :], NN)

        coupling = fold(gather(which, ref["gather%d" % which], known[...], use,
                               jnp.zeros((2 * count, pivot_block), jnp.float32)))
        pair = ref["pair%d" % level]
        pair[...] = split(ref["solved%d" % level][...] - coupling)

        def part(index, level=level, pair=pair):
            return fold(dot(pair[...], pivots[level, :, block_of(index, pivot_block)], NN))

        own = scatter(which + 1, ref["part%d" % (which + 1)], ref["land%d" % (which + 1)], part)
        own_pair, known_pair = split(own), split(known[...])

        def child(side):
            return fold(dot(own_pair, tables[level, side, :pivot_block, :], NN)
                        + dot(known_pair, tables[level, side, pivot_block:, :], NN))

        ref["child%d" % level][...] = child(1)
        rows = block_of(bits[level], count)
        copy = swap(ref["child%d" % level], ref["known%d" % level].at[rows], levels + level, level)
        copy.start()
        swaps.append(copy)
        ref["own%d" % level][...] = own
        size = levels - 1 - level
        for g in range(1 << size):
            for k in range(group):
                pivot_out[0, pl.ds(offsets[level] + (k << size | bit_reverse(g, size)), 1), :] = (
                    ref["own%d" % level][pl.ds(g * group + k, 1), :])
        ref["known%d" % level][rows, :] = child(0)
        copy.wait_recv()

    known = ref["known0"]
    for g in range(1 << levels):
        for k in range(group):
            update_out[0, pl.ds(k << levels | bit_reverse(g, levels), 1), :] = known[pl.ds(g * group + k, 1), :]

    for copy in swaps:
        copy.wait_send()
    for which in range(4 * levels + 1):
        if "gather%d" % which in ref:
            buf = ref["gather%d" % which]
        else:
            buf = ref["part%d" % which]

        def finish(slot, _, which=which, buf=buf):
            send(buf.at[slot], buf.at[slot], which, slot, {"panel": panel ^ 1}).wait_send()
            return _
        lax.fori_loop(1, panels, finish, 0)


def local(panels, pivot_rhs, subtree_update, lower_pivot, lower_update, row_map, root_inverse):
    levels = lower_pivot.shape[0]
    pivot_block, update_block = pivot_rhs.shape[2], subtree_update.shape[2]
    vectors = subtree_update.shape[1]
    outer = min(OUTER_MAX, panels)
    inner = panels // outer
    slots = pivot_block + update_block
    f32, bf16 = jnp.float32, jnp.bfloat16
    scratch = {
        "pivots": pltpu.VMEM((levels,) + lower_pivot.shape[2:], bf16),
        "updates": pltpu.VMEM((levels,) + lower_update.shape[2:], bf16),
        "root": pltpu.VMEM(root_inverse.shape, bf16),
        "tables": pltpu.VMEM((levels, 2, slots, update_block), bf16),
    }
    for level in range(levels):
        count = vectors >> (level + 1)
        back = 2 * levels + 1 + 2 * level
        scratch["current%d" % level] = pltpu.VMEM((2 * count, update_block), f32)
        scratch["known%d" % level] = pltpu.VMEM((2 * count, update_block), f32)
        scratch["swapped%d" % level] = pltpu.VMEM((count, update_block), f32)
        scratch["child%d" % level] = pltpu.VMEM((count, update_block), f32)
        scratch["kept%d" % level] = pltpu.VMEM((count, update_block), f32)
        scratch["solved%d" % level] = pltpu.VMEM((count, pivot_block), f32)
        scratch["rhs%d" % level] = pltpu.VMEM((count, pivot_block), f32)
        scratch["own%d" % level] = pltpu.VMEM((count, pivot_block), f32)
        scratch["pair%d" % level] = pltpu.VMEM((2 * count, pivot_block), bf16)
        scratch["gather%d" % (2 * level)] = pltpu.VMEM((panels, count, pivot_block), f32)
        scratch["gather%d" % back] = pltpu.VMEM((panels, count, update_block), f32)
        for which, width in ((2 * level + 1, update_block), (back + 1, pivot_block)):
            scratch["part%d" % which] = pltpu.VMEM((panels, count, width), f32)
            scratch["land%d" % which] = pltpu.VMEM((panels, count, width), f32)
    count = vectors >> levels
    scratch["current%d" % levels] = pltpu.VMEM((count, update_block), f32)
    scratch["known%d" % levels] = pltpu.VMEM((count, update_block), f32)
    scratch["gather%d" % (2 * levels)] = pltpu.VMEM((panels, count, update_block), f32)
    scratch["send_sem"] = pltpu.SemaphoreType.DMA((4 * levels + 1, panels))
    scratch["recv_sem"] = pltpu.SemaphoreType.DMA((4 * levels + 1, panels))
    scratch["swap_send_sem"] = pltpu.SemaphoreType.DMA((2 * levels,))
    scratch["swap_recv_sem"] = pltpu.SemaphoreType.DMA((2 * levels,))
    scratch["load_sem"] = pltpu.SemaphoreType.DMA((2 * levels + 1,))
    names = ["pivot_rhs", "subtree_update", "row_map", "lower_pivot", "lower_update", "root_inverse",
             "pivot_solution", "subtree_solution"] + list(scratch)
    vmem, anywhere = pl.BlockSpec(memory_space=pltpu.VMEM), pl.BlockSpec(memory_space=pl.ANY)
    return pl.pallas_call(
        functools.partial(kernel, levels, outer, inner, names),
        out_shape=(jax.ShapeDtypeStruct(pivot_rhs.shape, f32),
                   jax.ShapeDtypeStruct(subtree_update.shape, f32)),
        in_specs=[vmem] * 3 + [anywhere] * 3,
        out_specs=(vmem, vmem),
        scratch_shapes=list(scratch.values()),
        compiler_params=pltpu.CompilerParams(collective_id=0, has_side_effects=True),
    )(pivot_rhs, subtree_update, row_map, lower_pivot, lower_update, root_inverse)


def solution(mesh):
    in_specs = (
        P("leaf", None, "panel"),
        P("leaf", None, "panel"),
        P(None, "leaf", "panel", None),
        P(None, "leaf", None, "panel"),
        P(None, "leaf", None, "panel"),
        P("panel", None),
    )
    out_specs = (P("leaf", None, "panel"), P("leaf", None, "panel"))
    return jax.shard_map(functools.partial(local, mesh.shape["panel"]), mesh=mesh, in_specs=in_specs,
                         out_specs=out_specs, check_vma=False)
```

time: 491 us -> 110 us (0.22)
  waiting for transfers between devices: 251 us -> 0 us
  blocking collectives: 157 us -> 0 us
  Pallas kernels: 0 us -> 106 us
  matrix products: 56.8 us -> 0 us
  between operations: 13.9 us -> 0.64 us
  other arithmetic: 4.96 us -> 0 us
    reduce_scatter x4 -> x0, waiting for transfers between devices: 246 us -> none  [the longest x2 124 us: local(): lax.psum_scatter(lax.dot_general(factor_rows, solved, CONTRACT_LAST, prec...]
    all_gather x5 -> x0, blocking collectives: 157 us -> none  [the longest x2 64 us: local(): lax.all_gather(right_side, 'panel', axis=1, tiled=True)]
    pallas_call x0 -> x1, Pallas kernels: none -> 106 us  [local(): pl.pallas_call(functools.partial(kernel, levels, outer, inner, names), ou...]
    dot_general x13 -> x0, matrix products: 56.8 us -> none  [the longest x2 12.9 us: local(): lax.dot_general(factor_rows, solved, CONTRACT_LAST, precision=HIGHEST_PRE...]
    ppermute x4 -> x0, waiting for transfers between devices: 5 us -> none  [partner(): lax.ppermute(value, axis, [(i, i ^ 1 << stride) for i in range(lax.axis_s...]
  transfers between devices with their start and end apart: 8 -> 0, of which waited for: 7 -> 0; matrix products, arithmetic and copies ran while one was open for 0% -> 0% of each run, Pallas kernels for 0% -> 0%
where the time goes in v1:
time: 110 us
  Pallas kernels  106 us (96%)
  local copies, waits for them, and re-layouts  3.11 us (3%)
    pallas_call x1, Pallas kernels, local(): pl.pallas_call(functools.partial(kernel, levels, outer, inner, names), ou...  106 us
    unnamed x2, local copies, waits for them, and re-layouts  3.11 us

profile of v1, /device:TPU:0, one launch (start us, length us, event | category | flops | bytes accessed | tf_op | source)
XLA Modules:
  0.0 109.6 jit_solution(704187446806611873)
XLA Ops:
  0.6 105.8 %shard_map.77 = (f32[1,48,512]{2,1,0:T(8,128)}, f32[1,64,512]{2,1,0:T(8,128)}) custom-call(f32[1,48,512]{2,1,0:T(8,128)} %args_0_.4, f32[1,64,512]{2,1,0:T(8,128)} %args_1_.4, s32[2,1,2,512]{3,2,1,0:T(2,128)} %args_2_.4, bf16[2,1,512,4096]{3,2,1,0:T(8,128)(2,1)} %args_3_.4, bf16[2,1,4096,512]{3,2,1,0:T(8,128)(2,1)} %args_4_.4, bf16[512,4096]{1,0:T(8,128)(2,1)} %args_5_.4), custom_call_target="tpu_custom_call" | custom-call | tf_op jit(solution)/shard_map/pallas_call | solution.py:339
  106.5 1.5 %copy.10 = f32[1,48,512]{2,1,0:T(8,128)} copy(f32[1,48,512]{2,1,0:T(8,128)} %get-tuple-element.4) | data formatting | bytes 196608
  108.0 1.6 %copy.11 = f32[1,64,512]{2,1,0:T(8,128)} copy(f32[1,64,512]{2,1,0:T(8,128)} %get-tuple-element.5) | data formatting | bytes 262144

commit v2 on v1

v2 whole, which is shorter than its diff:
```python
import functools

import jax
import jax.numpy as jnp
from jax import lax
from jax.experimental import pallas as pl
from jax.experimental.pallas import tpu as pltpu
from jax.sharding import PartitionSpec as P

MESH = pl.DeviceIdType.MESH
OUTER_MAX = 4
DIRECT_FROM = 1
DIRECT_PANELS = 8
BATCHES = 2
NT = (((1,), (1,)), ((), ()))
NN = (((1,), (0,)), ((), ()))


def bit_reverse(value, bits):
    out = 0
    for i in range(bits):
        out |= (value >> i & 1) << (bits - 1 - i)
    return out


def split(x):
    high = x.astype(jnp.bfloat16).astype(jnp.float32)
    return jnp.concatenate([high, x - high], 0).astype(jnp.bfloat16)


def fold(x):
    half = x.shape[0] // 2
    return x[:half] + x[half:]


def dot(x, w, dims):
    return lax.dot_general(x, w, dims, preferred_element_type=jnp.float32)


def loop(low, high, step, carry):
    if high - low <= 8:
        for i in range(low, high):
            carry = step(i, carry)
        return carry
    return lax.fori_loop(low, high, step, carry)


def kernel(levels, batches, outer, inner, names, *args):
    ref = dict(zip(names, args))
    pivot_in, update_in, maps = ref["pivot_rhs"], ref["subtree_update"], ref["row_map"]
    pivot_out, update_out = ref["pivot_solution"], ref["subtree_solution"]
    pivots, updates, root = ref["pivots"], ref["updates"], ref["root"]
    panels = outer * inner
    pivot_block, update_block = pivot_in.shape[2], update_in.shape[2]
    whole_vectors = update_in.shape[1]
    vectors = whole_vectors // batches
    slots = pivot_block + update_block
    group = vectors >> levels

    leaf = lax.axis_index("leaf")
    panel = lax.axis_index("panel")
    row, col = panel // inner, panel % inner

    bits = [(leaf >> level) & 1 for level in range(levels)]
    counts = [vectors >> (level + 1) for level in range(levels)]
    offsets = [sum(whole_vectors >> (below + 1) for below in range(level)) for level in range(levels)]

    loads = []
    for level in range(levels):
        loads.append(pltpu.make_async_copy(
            ref["lower_pivot"].at[level, 0], pivots.at[level], ref["load_sem"].at[2 * level]))
        loads.append(pltpu.make_async_copy(
            ref["lower_update"].at[level, 0], updates.at[level], ref["load_sem"].at[2 * level + 1]))
    loads.append(pltpu.make_async_copy(ref["root_inverse"], root, ref["load_sem"].at[2 * levels]))
    for load in loads:
        load.start()

    barrier = pltpu.get_barrier_semaphore()
    for d in range(1, outer):
        pl.semaphore_signal(barrier, 1, device_id={"panel": (row ^ d) * inner + col}, device_id_type=MESH)
    for e in range(1, inner):
        pl.semaphore_signal(barrier, 1, device_id={"panel": row * inner + (col ^ e)}, device_id_type=MESH)
    if panels <= DIRECT_PANELS:
        for d in range(1, outer):
            for e in range(1, inner):
                pl.semaphore_signal(
                    barrier, 1, device_id={"panel": (row ^ d) * inner + (col ^ e)}, device_id_type=MESH)
    for level in range(levels):
        pl.semaphore_signal(barrier, 1, device_id={"leaf": leaf ^ (1 << level)}, device_id_type=MESH)

    for batch in range(batches):
        first = ref["current0@%d" % batch]
        for g in range(1 << levels):
            for k in range(group):
                first[pl.ds(g * group + k, 1), :] = update_in[0, pl.ds(batch * vectors + (k << levels | bit_reverse(g, levels)), 1), :]
        for level in range(levels):
            size = levels - 1 - level
            for g in range(1 << size):
                for k in range(group):
                    ref["rhs%d@%d" % (level, batch)][pl.ds(g * group + k, 1), :] = pivot_in[
                        0, pl.ds(offsets[level] + batch * counts[level] + (k << size | bit_reverse(g, size)), 1), :]
    met = panels - 1 if panels <= DIRECT_PANELS else outer - 1 + inner - 1
    pl.semaphore_wait(barrier, met + levels)

    row_order = [d for d in (1, 3, 2) if d < outer]
    far_order = [d for d in (3, 2, 1) if d < outer]

    def place(d, e):
        return (row ^ d) * inner + (col ^ e)

    def send(source, target, which, slot, device):
        batch, which = which
        return pltpu.make_async_remote_copy(
            src_ref=source, dst_ref=target, send_sem=ref["send_sem"].at[batch, which, slot],
            recv_sem=ref["recv_sem"].at[batch, which, slot], device_id=device, device_id_type=MESH)

    def to_row(source, target, which, slot, d):
        return send(source, target, which, slot, {"panel": (row ^ d) * inner + col})

    def to_col(source, target, which, slot, e):
        return send(source, target, which, slot, {"panel": row * inner + (col ^ e)})

    def direct(which):
        which = which[1]
        level = which // 2 if which <= 2 * levels else (which - 2 * levels - 1) // 2
        return level >= DIRECT_FROM and panels <= DIRECT_PANELS

    def to_any(source, target, which, slot, device):
        return send(source, target, which, slot, {"panel": device})

    def gather_direct(which, buf, value, use, acc):
        buf[0] = value

        def go(i, _):
            slot = panels - 1 - i
            to_any(buf.at[0], buf.at[slot], which, slot, place(slot // inner, slot % inner)).start()
            return _
        loop(0, panels - 1, go, 0)
        acc = use(acc, buf[0], place(0, 0))
        yield

        def take(slot, acc):
            index = place(slot // inner, slot % inner)
            to_any(buf.at[slot], buf.at[slot], which, slot, index).wait_recv()
            return use(acc, buf[slot], index)
        return loop(1, panels, take, acc)

    def scatter_direct(which, part_buf, in_buf, part):
        def go(i, _):
            slot = panels - 1 - i
            index = place(slot // inner, slot % inner)
            part_buf[slot] = part(index)
            to_any(part_buf.at[slot], in_buf.at[slot], which, slot, index).start()
            return _
        loop(0, panels - 1, go, 0)
        own = part(place(0, 0))
        yield

        def take(slot, acc):
            index = place(slot // inner, slot % inner)
            to_any(in_buf.at[slot], in_buf.at[slot], which, slot, index).wait_recv()
            return acc + in_buf[slot]
        return loop(1, panels, take, own)

    def gather(which, buf, value, use, acc):
        if direct(which):
            return (yield from gather_direct(which, buf, value, use, acc))
        buf[0] = value
        for d in far_order:
            to_row(buf.at[0], buf.at[d * inner], which, d * inner, d).start()

        def forward(d):
            def go(e, _):
                to_col(buf.at[d * inner], buf.at[d * inner + e], which, d * inner + e, e).start()
                return _
            loop(1, inner, go, 0)

        def arrived(d, acc):
            def go(e, acc):
                slot = d * inner + e
                to_col(buf.at[slot], buf.at[slot], which, slot, e).wait_recv()
                return use(acc, buf[slot], place(d, e))
            return loop(1, inner, go, acc)

        forward(0)
        acc = use(acc, buf[0], place(0, 0))
        yield
        last = 0
        for d in row_order:
            to_row(buf.at[d * inner], buf.at[d * inner], which, d * inner, d).wait_recv()
            forward(d)
            acc = use(acc, buf[d * inner], place(d, 0))
            acc = arrived(last, acc)
            last = d
        yield
        return arrived(last, acc)

    def scatter(which, part_buf, in_buf, part):
        if direct(which):
            return (yield from scatter_direct(which, part_buf, in_buf, part))
        for d in far_order + [0]:
            def go(e, _, d=d):
                slot = d * inner + e
                part_buf[slot] = part(place(d, e))
                to_col(part_buf.at[slot], in_buf.at[slot], which, slot, e).start()
                return _
            loop(1, inner, go, 0)

        yield

        def collect(d):
            def go(e, acc):
                slot = d * inner + e
                to_col(in_buf.at[slot], in_buf.at[slot], which, slot, e).wait_recv()
                return acc + in_buf[slot]
            return loop(1, inner, go, part(place(d, 0)))

        for d in far_order:
            slot = d * inner
            part_buf[slot] = collect(d)
            to_row(part_buf.at[slot], in_buf.at[slot], which, slot, d).start()
        acc = collect(0)
        yield
        for d in row_order:
            slot = d * inner
            to_row(in_buf.at[slot], in_buf.at[slot], which, slot, d).wait_recv()
            acc = acc + in_buf[slot]
        return acc

    def swap(source, target, which, level):
        return pltpu.make_async_remote_copy(
            src_ref=source, dst_ref=target, send_sem=ref["swap_send_sem"].at[which[0], which[1]],
            recv_sem=ref["swap_recv_sem"].at[which[0], which[1]], device_id={"leaf": leaf ^ (1 << level)},
            device_id_type=MESH)

    def block_of(index, size):
        return pl.ds(pl.multiple_of(index * size, size), size)

    swaps = []

    def begin_swap(level, batch):
        count = counts[level]
        copy = swap(ref["current%d@%d" % (level, batch)].at[block_of(1 - bits[level], count)],
                    ref["swapped%d@%d" % (level, batch)], (batch, level), level)
        copy.start()
        swaps.append(copy)
        return copy

    loaded = set()

    def ready(index):
        if index not in loaded:
            loaded.add(index)
            loads[index].wait()

    tables = ref["tables"]

    def run(batch):
        for level in range(levels):
            count = counts[level]
            current = ref["current%d@%d" % (level, batch)]
            copy = begin_swap(level, batch)
            yield
            total = dot(split(current[block_of(bits[level], count), :]), tables[level, 0], NT)
            copy.wait_recv()
            total = total + dot(split(ref["swapped%d@%d" % (level, batch)][...]), tables[level, 1], NT)
            assembled = fold(total)
            ref["kept%d@%d" % (level, batch)][...] = assembled[:, pivot_block:]
            ready(2 * level)

            def use(acc, value, index, level=level):
                return acc + dot(split(value), pivots[level, :, block_of(index, pivot_block)], NT)

            solved = fold((yield from gather((batch, 2 * level), ref["gather%d@%d" % (2 * level, batch)],
                                 ref["rhs%d@%d" % (level, batch)][...] + assembled[:, :pivot_block], use, jnp.zeros((2 * count, pivot_block), jnp.float32))))
            ref["solved%d@%d" % (level, batch)][...] = solved
            pair = ref["pair%d@%d" % (level, batch)]
            pair[...] = split(solved)
            ready(2 * level + 1)

            def part(index, level=level, pair=pair):
                return fold(dot(pair[...], updates[level, block_of(index, update_block), :], NT))

            coupled = yield from scatter((batch, 2 * level + 1), ref["part%d@%d" % (2 * level + 1, batch)], ref["land%d@%d" % (2 * level + 1, batch)], part)
            ref["current%d@%d" % (level + 1, batch)][...] = ref["kept%d@%d" % (level, batch)][...] - coupled

        ready(2 * levels)
        count = counts[levels - 1]

        def use_root(acc, value, index):
            return acc + dot(split(value), root[:, block_of(index, update_block)], NT)

        known = fold((yield from gather((batch, 2 * levels), ref["gather%d@%d" % (2 * levels, batch)], ref["current%d@%d" % (levels, batch)][...],
                            use_root, jnp.zeros((2 * count, update_block), jnp.float32))))
        ref["known%d@%d" % (levels, batch)][...] = known

        for level in range(levels - 1, -1, -1):
            count = counts[level]
            which = 2 * levels + 1 + 2 * level
            known = ref["known%d@%d" % (level + 1, batch)]

            def use(acc, value, index, level=level):
                return acc + dot(split(value), updates[level, block_of(index, update_block), :], NN)

            coupling = fold((yield from gather((batch, which), ref["gather%d@%d" % (which, batch)], known[...], use,
                                   jnp.zeros((2 * count, pivot_block), jnp.float32))))
            pair = ref["pair%d@%d" % (level, batch)]
            pair[...] = split(ref["solved%d@%d" % (level, batch)][...] - coupling)

            def part(index, level=level, pair=pair):
                return fold(dot(pair[...], pivots[level, :, block_of(index, pivot_block)], NN))

            own = yield from scatter((batch, which + 1), ref["part%d@%d" % (which + 1, batch)], ref["land%d@%d" % (which + 1, batch)], part)
            own_pair, known_pair = split(own), split(known[...])

            def child(side):
                return fold(dot(own_pair, tables[level, side, :pivot_block, :], NN)
                            + dot(known_pair, tables[level, side, pivot_block:, :], NN))

            ref["child%d@%d" % (level, batch)][...] = child(1)
            rows = block_of(bits[level], count)
            copy = swap(ref["child%d@%d" % (level, batch)], ref["known%d@%d" % (level, batch)].at[rows], (batch, levels + level), level)
            copy.start()
            swaps.append(copy)
            ref["own%d@%d" % (level, batch)][...] = own
            size = levels - 1 - level
            for g in range(1 << size):
                for k in range(group):
                    pivot_out[0, pl.ds(offsets[level] + batch * count + (k << size | bit_reverse(g, size)), 1), :] = (
                        ref["own%d@%d" % (level, batch)][pl.ds(g * group + k, 1), :])
            ref["known%d@%d" % (level, batch)][rows, :] = child(0)
            yield
            copy.wait_recv()

        known = ref["known0@%d" % batch]
        for g in range(1 << levels):
            for k in range(group):
                update_out[0, pl.ds(batch * vectors + (k << levels | bit_reverse(g, levels)), 1), :] = known[pl.ds(g * group + k, 1), :]

    runs = [run(batch) for batch in range(batches)]
    for one in runs:
        next(one)
    chunk = min(128, slots)
    for level in range(levels):
        for side in range(2):
            child = bits[level] if side == 0 else 1 - bits[level]
            target = maps[level, 0, pl.ds(child, 1), :]

            def fill(i, _, level=level, side=side, target=target):
                rows = lax.broadcasted_iota(jnp.int32, (chunk, update_block), 0) + i * chunk
                ref["tables"][level, side, block_of(i, chunk), :] = jnp.where(
                    rows == target, 1.0, 0.0).astype(jnp.bfloat16)
                return _
            lax.fori_loop(0, slots // chunk, fill, 0)

    while runs:
        runs = [one for one in runs if next(one, True) is None]

    for copy in swaps:
        copy.wait_send()
    for which in range(4 * levels + 1):
        for batch in range(batches):
            name = "gather%d@%d" % (which, batch)
            buf = ref[name] if name in ref else ref["part%d@%d" % (which, batch)]

            def finish(slot, _, which=which, batch=batch, buf=buf):
                send(buf.at[slot], buf.at[slot], (batch, which), slot, {"panel": panel ^ 1}).wait_send()
                return _
            lax.fori_loop(1, panels, finish, 0)


def local(panels, pivot_rhs, subtree_update, lower_pivot, lower_update, row_map, root_inverse):
    levels = lower_pivot.shape[0]
    pivot_block, update_block = pivot_rhs.shape[2], subtree_update.shape[2]
    batches = BATCHES if subtree_update.shape[1] >> levels >= 8 * BATCHES else 1
    vectors = subtree_update.shape[1] // batches
    outer = min(OUTER_MAX, panels)
    inner = panels // outer
    slots = pivot_block + update_block
    f32, bf16 = jnp.float32, jnp.bfloat16
    scratch = {
        "pivots": pltpu.VMEM((levels,) + lower_pivot.shape[2:], bf16),
        "updates": pltpu.VMEM((levels,) + lower_update.shape[2:], bf16),
        "root": pltpu.VMEM(root_inverse.shape, bf16),
        "tables": pltpu.VMEM((levels, 2, slots, update_block), bf16),
    }
    for batch in range(batches):
        for level in range(levels):
            count = vectors >> (level + 1)
            back = 2 * levels + 1 + 2 * level
            scratch["current%d@%d" % (level, batch)] = pltpu.VMEM((2 * count, update_block), f32)
            scratch["known%d@%d" % (level, batch)] = pltpu.VMEM((2 * count, update_block), f32)
            scratch["swapped%d@%d" % (level, batch)] = pltpu.VMEM((count, update_block), f32)
            scratch["child%d@%d" % (level, batch)] = pltpu.VMEM((count, update_block), f32)
            scratch["kept%d@%d" % (level, batch)] = pltpu.VMEM((count, update_block), f32)
            scratch["solved%d@%d" % (level, batch)] = pltpu.VMEM((count, pivot_block), f32)
            scratch["rhs%d@%d" % (level, batch)] = pltpu.VMEM((count, pivot_block), f32)
            scratch["own%d@%d" % (level, batch)] = pltpu.VMEM((count, pivot_block), f32)
            scratch["pair%d@%d" % (level, batch)] = pltpu.VMEM((2 * count, pivot_block), bf16)
            scratch["gather%d@%d" % (2 * level, batch)] = pltpu.VMEM((panels, count, pivot_block), f32)
            scratch["gather%d@%d" % (back, batch)] = pltpu.VMEM((panels, count, update_block), f32)
            for which, width in ((2 * level + 1, update_block), (back + 1, pivot_block)):
                scratch["part%d@%d" % (which, batch)] = pltpu.VMEM((panels, count, width), f32)
                scratch["land%d@%d" % (which, batch)] = pltpu.VMEM((panels, count, width), f32)
        count = vectors >> levels
        scratch["current%d@%d" % (levels, batch)] = pltpu.VMEM((count, update_block), f32)
        scratch["known%d@%d" % (levels, batch)] = pltpu.VMEM((count, update_block), f32)
        scratch["gather%d@%d" % (2 * levels, batch)] = pltpu.VMEM((panels, count, update_block), f32)
    scratch["send_sem"] = pltpu.SemaphoreType.DMA((batches, 4 * levels + 1, panels))
    scratch["recv_sem"] = pltpu.SemaphoreType.DMA((batches, 4 * levels + 1, panels))
    scratch["swap_send_sem"] = pltpu.SemaphoreType.DMA((batches, 2 * levels))
    scratch["swap_recv_sem"] = pltpu.SemaphoreType.DMA((batches, 2 * levels))
    scratch["load_sem"] = pltpu.SemaphoreType.DMA((2 * levels + 1,))
    names = ["pivot_rhs", "subtree_update", "row_map", "lower_pivot", "lower_update", "root_inverse",
             "pivot_solution", "subtree_solution"] + list(scratch)
    vmem, anywhere = pl.BlockSpec(memory_space=pltpu.VMEM), pl.BlockSpec(memory_space=pl.ANY)
    return pl.pallas_call(
        functools.partial(kernel, levels, batches, outer, inner, names),
        out_shape=(jax.ShapeDtypeStruct(pivot_rhs.shape, f32),
                   jax.ShapeDtypeStruct(subtree_update.shape, f32)),
        in_specs=[vmem] * 3 + [anywhere] * 3,
        out_specs=(vmem, vmem),
        scratch_shapes=list(scratch.values()),
        compiler_params=pltpu.CompilerParams(collective_id=0, has_side_effects=True),
    )(pivot_rhs, subtree_update, row_map, lower_pivot, lower_update, root_inverse)


def solution(mesh):
    in_specs = (
        P("leaf", None, "panel"),
        P("leaf", None, "panel"),
        P(None, "leaf", "panel", None),
        P(None, "leaf", None, "panel"),
        P(None, "leaf", None, "panel"),
        P("panel", None),
    )
    out_specs = (P("leaf", None, "panel"), P("leaf", None, "panel"))
    return jax.shard_map(functools.partial(local, mesh.shape["panel"]), mesh=mesh, in_specs=in_specs,
                         out_specs=out_specs, check_vma=False)
```

time: 110 us -> 94.3 us (0.86)
  Pallas kernels: 106 us -> 90.4 us
    pallas_call x1, Pallas kernels: 106 us -> 90.4 us  [local(): pl.pallas_call(functools.partial(kernel, levels, batches, outer, inner, n...]
where the time goes in v2:
time: 94.3 us; the launch traced here: 94.2 us
  Pallas kernels  90.4 us (96%)
  local copies, waits for them, and re-layouts  3.11 us (3%)
    pallas_call x1, Pallas kernels, local(): pl.pallas_call(functools.partial(kernel, levels, batches, outer, inner, n...  90.4 us
    unnamed x2, local copies, waits for them, and re-layouts  3.11 us

profile of v2, /device:TPU:0, one launch (start us, length us, event | category | flops | bytes accessed | tf_op | source)
XLA Modules:
  0.0 94.2 jit_solution(634076897412740947)
XLA Ops:
  0.6 90.4 %shard_map.77 = (f32[1,48,512]{2,1,0:T(8,128)}, f32[1,64,512]{2,1,0:T(8,128)}) custom-call(f32[1,48,512]{2,1,0:T(8,128)} %args_0_.4, f32[1,64,512]{2,1,0:T(8,128)} %args_1_.4, s32[2,1,2,512]{3,2,1,0:T(2,128)} %args_2_.4, bf16[2,1,512,4096]{3,2,1,0:T(8,128)(2,1)} %args_3_.4, bf16[2,1,4096,512]{3,2,1,0:T(8,128)(2,1)} %args_4_.4, bf16[512,4096]{1,0:T(8,128)(2,1)} %args_5_.4), custom_call_target="tpu_custom_call" | custom-call | tf_op jit(solution)/shard_map/pallas_call | solution.py:417
  91.0 1.5 %copy.10 = f32[1,48,512]{2,1,0:T(8,128)} copy(f32[1,48,512]{2,1,0:T(8,128)} %get-tuple-element.4) | data formatting | bytes 196608
  92.6 1.6 %copy.11 = f32[1,64,512]{2,1,0:T(8,128)} copy(f32[1,64,512]{2,1,0:T(8,128)} %get-tuple-element.5) | data formatting | bytes 262144

commit v3 on v2

--- a/solution.py
+++ b/solution.py
@@ -121,9 +121,11 @@
         return send(source, target, which, slot, {"panel": row * inner + (col ^ e)})
 
     def direct(which):
-        which = which[1]
-        level = which // 2 if which <= 2 * levels else (which - 2 * levels - 1) // 2
-        return level >= DIRECT_FROM and panels <= DIRECT_PANELS
+        batch, which = which
+        back = which > 2 * levels
+        level = (which - 2 * levels - 1) // 2 if back else which // 2
+        adds = (which - back) % 2 == 1
+        return (level >= DIRECT_FROM or not adds) and panels <= DIRECT_PANELS
 
     def to_any(source, target, which, slot, device):
         return send(source, target, which, slot, {"panel": device})

time: 94.3 us -> 93 us (0.986)
  Pallas kernels: 90.4 us -> 89 us
    pallas_call x1, Pallas kernels: 90.4 us -> 89 us  [local(): pl.pallas_call(functools.partial(kernel, levels, batches, outer, inner, n...]
where the time goes in v3:
time: 93 us; the launch traced here: 92.8 us
  Pallas kernels  89 us (96%)
  local copies, waits for them, and re-layouts  3.11 us (3%)
    pallas_call x1, Pallas kernels, local(): pl.pallas_call(functools.partial(kernel, levels, batches, outer, inner, n...  89 us
    unnamed x2, local copies, waits for them, and re-layouts  3.11 us

profile of v3, /device:TPU:0, one launch (start us, length us, event | category | flops | bytes accessed | tf_op | source)
XLA Modules:
  0.0 92.8 jit_solution(4584643093451538151)
XLA Ops:
  0.6 89.0 %shard_map.77 = (f32[1,48,512]{2,1,0:T(8,128)}, f32[1,64,512]{2,1,0:T(8,128)}) custom-call(f32[1,48,512]{2,1,0:T(8,128)} %args_0_.4, f32[1,64,512]{2,1,0:T(8,128)} %args_1_.4, s32[2,1,2,512]{3,2,1,0:T(2,128)} %args_2_.4, bf16[2,1,512,4096]{3,2,1,0:T(8,128)(2,1)} %args_3_.4, bf16[2,1,4096,512]{3,2,1,0:T(8,128)(2,1)} %args_4_.4, bf16[512,4096]{1,0:T(8,128)(2,1)} %args_5_.4), custom_call_target="tpu_custom_call" | custom-call | tf_op jit(solution)/shard_map/pallas_call | solution.py:419
  89.7 1.5 %copy.10 = f32[1,48,512]{2,1,0:T(8,128)} copy(f32[1,48,512]{2,1,0:T(8,128)} %get-tuple-element.4) | data formatting | bytes 196608
  91.2 1.6 %copy.11 = f32[1,64,512]{2,1,0:T(8,128)} copy(f32[1,64,512]{2,1,0:T(8,128)} %get-tuple-element.5) | data formatting | bytes 262144
